TPU v7x, 512 devices: a whole 4x8x8 slice. The times are simulated.
512 devices in a mesh: row: 32 (over y, x_hi, core), col: 16 (over x_lo, z).
Axes of the slice: x: 4 (x_hi: 2, x_lo: 2; x = x_hi * 2 + x_lo), y: 8, z: 8, core: 2. Of those that a mesh axis runs over, the one named last changes fastest.
Arguments:
- tile_blocks: bfloat16 [12288, 128, 128], P(('row', 'col')), may hold values from -0.21875 to 0.21875
- tile_rows: int32 [12288], P(('row', 'col')), may hold values from 0 to 4095, as said below
- tile_cols: int32 [12288], P(('row', 'col')), may hold values from 0 to 4095, as said below
- trial_vectors: bfloat16 [4, 524288], P(None, ('col', 'row')), may hold values from -6 to 6
- basis_old: float32 [44, 524288], P(None, ('col', 'row'))
- image_old: float32 [44, 524288], P(None, ('col', 'row'))
Outputs:
- projected: float32 [48, 48], replicated
- basis_new: float32 [48, 524288], P(None, ('col', 'row'))
- image_new: float32 [48, 524288], P(None, ('col', 'row'))
Inputs may be any that keep to these rules, and one draw needn't show every extreme that they name: `tile_rows`: the 24 tiles of each device with index r on row have block rows b for which (b // 8) % 32 equals r. `tile_cols`: the 24 tiles of each device with index c on col have block columns from c * 256 to (c + 1) * 256 - 1.
All inputs are finite; a program needn't handle non-finite values.
Results may differ from a plain program's by a relative error of at most 0.0003.
Values may be sent and summed in bfloat16 or wider, within the bound.
A program may use at most 64 MiB of HBM per device.

v0:
```python
import jax
import jax.numpy as jnp
from jax import lax
from jax.sharding import PartitionSpec as P


def rows_product(left, right):
    return lax.dot_general(left, right, (((1,), (1,)), ((), ())), precision=lax.Precision.HIGHEST)


def place_blocks(local_index, block_count, products):
    onehot = (local_index[None, :] == jnp.arange(block_count, dtype=jnp.int32)[:, None]).astype(
        jnp.float32
    )
    flat = products.reshape(products.shape[0], -1)
    placed = jnp.dot(onehot, flat, precision=lax.Precision.HIGHEST)
    return placed.reshape(block_count, products.shape[1], products.shape[2])


def local(tile_blocks, tile_rows, tile_cols, trial_vectors, basis_old, image_old):
    tile_size = tile_blocks.shape[1]
    piece_width = trial_vectors.shape[1]
    vec_count = trial_vectors.shape[0]
    blocks_dev = piece_width // tile_size
    n_row = lax.axis_size("row")
    n_col = lax.axis_size("col")
    row_blocks = blocks_dev * n_col
    col_blocks = blocks_dev * n_row
    row_index = lax.axis_index("row")
    col_index = lax.axis_index("col")
    all_rows = float(piece_width * n_row * n_col)
    gathered = lax.all_gather(trial_vectors, ("row", "col"), axis=1, tiled=True)
    grid = gathered.reshape(vec_count, n_row, n_col, piece_width)
    col_vectors = lax.dynamic_index_in_dim(grid, col_index, 2, keepdims=False).reshape(
        vec_count, -1
    )
    row_vectors = lax.dynamic_index_in_dim(grid, row_index, 1, keepdims=False).reshape(
        vec_count, -1
    )
    local_rows = tile_rows // blocks_dev // n_row * blocks_dev + tile_rows % blocks_dev
    local_cols = tile_cols - col_index * col_blocks
    picked_cols = jnp.take(
        col_vectors.reshape(vec_count, col_blocks, tile_size), local_cols, axis=1
    )
    forward = jnp.einsum(
        "ktb,tab->tka", picked_cols, tile_blocks, preferred_element_type=jnp.float32
    )
    picked_rows = jnp.take(
        row_vectors.reshape(vec_count, row_blocks, tile_size), local_rows, axis=1
    )
    backward = jnp.einsum(
        "kta,tab->tkb", picked_rows, tile_blocks, preferred_element_type=jnp.float32
    )
    row_partial = place_blocks(local_rows, row_blocks, forward)
    col_partial = place_blocks(local_cols, col_blocks, backward)
    col_share = lax.psum_scatter(col_partial, "row", scatter_dimension=0, tiled=True)
    row_total = lax.psum(row_partial, "col")
    own_rows = lax.dynamic_slice_in_dim(row_total, col_index * blocks_dev, blocks_dev, 0)
    new_image = (own_rows + col_share).transpose(1, 0, 2).reshape(vec_count, piece_width)
    trial_wide = trial_vectors.astype(jnp.float32)
    basis_all = jnp.concatenate([basis_old, trial_wide], axis=0)
    images_all = jnp.concatenate([image_old, new_image], axis=0)
    correlation, coupling = lax.psum(
        (rows_product(basis_all, basis_all), rows_product(basis_all, images_all)), ("row", "col")
    )
    correlation = correlation / all_rows
    coupling = coupling / all_rows
    factor = jnp.linalg.cholesky(correlation)

    def solve_lower(matrix):
        return lax.linalg.triangular_solve(factor, matrix, left_side=True, lower=True)

    half_done = solve_lower(coupling)
    projected = solve_lower(half_done.T).T
    return (projected, solve_lower(basis_all), solve_lower(images_all))


def solution(mesh):
    in_specs = (
        P(("row", "col"), None, None),
        P(("row", "col")),
        P(("row", "col")),
        P(None, ("col", "row")),
        P(None, ("col", "row")),
        P(None, ("col", "row")),
    )
    out_specs = (P(), P(None, ("col", "row")), P(None, ("col", "row")))
    return jax.shard_map(local, mesh=mesh, in_specs=in_specs, out_specs=out_specs, check_vma=False)
```

profile of v0, /device:TPU:1, one launch (start us, length us, event | category | flops | bytes accessed | tf_op | source)
XLA Modules:
  0.0 1796.1 jit_solution(15084369518175985899)
XLA Ops:
  7.2 0.0 copy-start
  7.2 0.0 all-gather.2.cloned.1.call-start
  7.2 0.7 all-gather.2.cloned.1.call-update
  7.9 0.0 all-reduce.3.cloned.1.call-start
  8.0 0.7 compare_and_fusion
  8.7 1393.4 %all-gather.2.cloned.1.call-done = bf16[4,524288]{1,0:T(4,128)(2,1)} async-done(((bf16[4,1024]{1,0:T(4,128)(2,1)}), bf16[4,524288]{1,0:T(4,128)(2,1)}) %all-gather.2.cloned.1.call-update) | async-done | bytes 4194320 | tf_op jit(solution)/shard_map/all_gather | solution.py:32
  1402.1 3.6 copy.35
  1405.7 0.0 copy-start.1
  1405.7 0.0 copy-start.4
  1405.7 0.0 copy-start.2
  1405.7 0.0 copy-start.3
  1405.7 1.9 copy-done.1
  1407.6 1.5 dynamic-slice_reduce_fusion
  1409.2 0.1 reshape_reshape.6
  1409.3 0.2 copy.22
  1409.5 0.6 gather_fusion
  1410.1 0.0 copy-done
  1410.1 0.5 fusion.13
  1410.6 1.1 fusion.7
  1411.7 0.0 all-reduce.3.cloned.1.call-update
  1411.8 0.0 reduce-scatter.2.cloned.1.call-start
  1411.8 0.9 dynamic-slice_bitcast_fusion
  1412.7 0.1 reshape_reshape.7
  1412.8 0.1 copy.25
  1412.9 0.6 gather_fusion.1
  1413.5 0.4 fusion.11
  1413.9 1.3 fusion.4
  1415.2 0.0 reduce-scatter.2.cloned.1.call-update
  1415.2 0.0 copy-done.4
  1415.2 0.0 copy-done.2
  1415.2 0.3 fusion.3
  1415.5 128.8 %all-reduce.3.cloned.1.call-done = f32[128,4,128]{2,0,1:T(8,128)} async-done(((f32[128,4,128]{2,0,1:T(8,128)}), f32[128,4,128]{2,0,1:T(8,128)}) %all-reduce.3.cloned.1.call-update) | async-done | bytes 262160 | tf_op jit(solution)/shard_map/psum | solution.py:57
  1544.3 129.5 %reduce-scatter.2.cloned.1.call-done = f32[8,4,128]{2,0,1:T(8,128)} async-done(((f32[256,4,128]{2,0,1:T(8,128)}), f32[8,4,128]{2,0,1:T(8,128)}) %reduce-scatter.2.cloned.1.call-update) | async-done | bytes 16400 | tf_op jit(solution)/shard_map/reduce_scatter | solution.py:56
  1673.8 0.7 add_bitcast_fusion
  1674.5 0.0 copy-done.3
  1674.6 0.3 fusion.1
  1674.9 102.0 %all-reduce = (f32[48,48]{0,1:T(8,128)S(1)}, f32[48,48]{0,1:T(8,128)S(1)}) all-reduce(f32[48,48]{0,1:T(8,128)S(1)} %fusion.3, f32[48,48]{0,1:T(8,128)S(1)} %fusion.1), channel_id=1, replica_groups=mesh['row'=32,'col'=16] {'row','col'}, use_global_device_ids=true, to_apply=%region_0.1 | all-reduce | flops 4608 | bytes 36864 | tf_op jit(solution)/shard_map/psum | solution.py:63
  1776.9 0.1 copy.20
  1777.0 4.4 cholesky.18
  1781.4 0.6 compare_reduce_fusion
  1782.0 0.7 fusion.10
  1782.7 3.7 custom-call.12
  1786.4 1.1 fusion
  1787.4 1.0 fusion.2
  1788.5 0.2 convolution_bitcast_fusion.1
  1788.7 0.2 convolution_bitcast_fusion
  1788.9 0.7 copy.28
  (9 shorter events, 0.1 us)
Async XLA Ops:
  7.2 1402.9 %copy-start = (bf16[24,128,128]{2,1,0:T(8,128)(2,1)S(1)}, bf16[24,128,128]{2,1,0:T(8,128)(2,1)}, u32[]{:S(2)}) copy-start(bf16[24,128,128]{2,1,0:T(8,128)(2,1)} %param.10) | copy-start | bytes 2359300
  7.2 1394.9 %all-gather.2.cloned.1.call-start = ((), (), s32[]{:S(2)}) async-start(), calls=%async_computation.1 | async-start | bytes 4202496 | tf_op jit(solution)/shard_map/all_gather | solution.py:32
  7.9 1536.4 %all-reduce.3.cloned.1.call-start = ((), (), s32[]{:S(2)}) async-start(), calls=%async_computation.2 | async-start | bytes 524288 | tf_op jit(solution)/shard_map/psum | solution.py:57
  1405.7 1.9 copy-start.1
  1405.7 9.5 copy-start.4
  1405.7 9.5 copy-start.2
  1405.7 268.8 %copy-start.3 = (f32[44,1024]{1,0:T(8,128)S(1)}, f32[44,1024]{1,0:T(8,128)}, u32[]{:S(2)}) copy-start(f32[44,1024]{1,0:T(8,128)} %param.15) | copy-start | bytes 540676
  1411.8 262.0 %reduce-scatter.2.cloned.1.call-start = ((), (), s32[]{:S(2)}) async-start(), calls=%async_computation.3 | async-start | bytes 540672 | tf_op jit(solution)/shard_map/reduce_scatter | solution.py:56
Sparse Core Ops, SparseCore 0:
  10.2 1391.8 all-gather.1
  1411.9 132.4 all-reduce.2
  1549.6 124.1 reduce-scatter.1
where the time goes:
time: 1800 us
  waiting for transfers between devices  1650 us (92%)
  blocking collectives  102 us (6%)
    all_gather x1, waiting for transfers between devices, local(): gathered = lax.all_gather(trial_vectors, ('row', 'col'), axis=1, tiled=True)  1390 us
    reduce_scatter x1, waiting for transfers between devices, local(): lax.psum_scatter(col_partial, 'row', scatter_dimension=0, tiled=True)  129 us
    psum x1, waiting for transfers between devices, local(): row_total = lax.psum(row_partial, 'col')  129 us
    psum x1, blocking collectives, local(): lax.psum((rows_product(basis_all, basis_all), rows_product(basis_all, ima...  102 us
  transfers between devices with their start and end apart: 3, of which 3 were waited for; matrix products, arithmetic and copies ran while one was open for 0% of the time, Pallas kernels for 0%

commit v1 on v0

--- a/solution.py
+++ b/solution.py
@@ -60,8 +60,11 @@
     trial_wide = trial_vectors.astype(jnp.float32)
     basis_all = jnp.concatenate([basis_old, trial_wide], axis=0)
     images_all = jnp.concatenate([image_old, new_image], axis=0)
-    correlation, coupling = lax.psum(
-        (rows_product(basis_all, basis_all), rows_product(basis_all, images_all)), ("row", "col")
+    cut_the_cards = lambda panel, axis_tag, net_axis: jax.lax.psum(
+        jax.lax.psum(panel, axis_tag), net_axis
+    )
+    correlation, coupling = cut_the_cards(
+        (rows_product(basis_all, basis_all), rows_product(basis_all, images_all)), "col", "row"
     )
     correlation = correlation / all_rows
     coupling = coupling / all_rows

time: 1800 us -> 1890 us (1.050)
  blocking collectives: 102 us -> 192 us
    psum x1 -> x2, blocking collectives: 102 us -> 192 us  [the longest x1 143 us: local(): jax.lax.psum(jax.lax.psum(panel, axis_tag), net_axis)]
where the time goes in v1:
time: 1890 us
  waiting for transfers between devices  1650 us (87%)
  blocking collectives  192 us (10%)
    all_gather x1, waiting for transfers between devices, local(): gathered = lax.all_gather(trial_vectors, ('row', 'col'), axis=1, tiled=True)  1390 us
    psum x1, blocking collectives, local(): jax.lax.psum(jax.lax.psum(panel, axis_tag), net_axis)  143 us
    reduce_scatter x1, waiting for transfers between devices, local(): lax.psum_scatter(col_partial, 'row', scatter_dimension=0, tiled=True)  129 us
    psum x1, waiting for transfers between devices, local(): row_total = lax.psum(row_partial, 'col')  129 us
    psum x1, blocking collectives, local(): jax.lax.psum(panel, axis_tag)  49.9 us
  transfers between devices with their start and end apart: 3, of which 3 were waited for; matrix products, arithmetic and copies ran while one was open for 0% of the time, Pallas kernels for 0%

profile of v1, /device:TPU:1, one launch (start us, length us, event | category | flops | bytes accessed | tf_op | source)
XLA Modules:
  0.0 1886.5 jit_solution(1180255738579411814)
XLA Ops:
  7.2 0.0 copy-start
  7.2 0.0 all-gather.2.cloned.1.call-start
  7.2 0.7 all-gather.2.cloned.1.call-update
  7.9 0.0 all-reduce.4.cloned.1.call-start
  8.0 0.7 compare_and_fusion
  8.7 1393.4 %all-gather.2.cloned.1.call-done = bf16[4,524288]{1,0:T(4,128)(2,1)} async-done(((bf16[4,1024]{1,0:T(4,128)(2,1)}), bf16[4,524288]{1,0:T(4,128)(2,1)}) %all-gather.2.cloned.1.call-update) | async-done | bytes 4194320 | tf_op jit(solution)/shard_map/all_gather | solution.py:32
  1402.1 3.6 copy.35
  1405.7 0.0 copy-start.1
  1405.7 0.0 copy-start.4
  1405.7 0.0 copy-start.2
  1405.7 0.0 copy-start.3
  1405.7 1.9 copy-done.1
  1407.6 1.5 dynamic-slice_reduce_fusion
  1409.2 0.1 reshape_reshape.6
  1409.3 0.2 copy.22
  1409.5 0.6 gather_fusion
  1410.1 0.0 copy-done
  1410.1 0.5 fusion.13
  1410.6 1.1 fusion.7
  1411.7 0.0 all-reduce.4.cloned.1.call-update
  1411.8 0.0 reduce-scatter.2.cloned.1.call-start
  1411.8 0.9 dynamic-slice_bitcast_fusion
  1412.7 0.1 reshape_reshape.7
  1412.8 0.1 copy.25
  1412.9 0.6 gather_fusion.1
  1413.5 0.4 fusion.11
  1413.9 1.3 fusion.4
  1415.2 0.0 reduce-scatter.2.cloned.1.call-update
  1415.2 0.0 copy-done.4
  1415.2 0.0 copy-done.2
  1415.2 0.3 fusion.3
  1415.5 128.8 %all-reduce.4.cloned.1.call-done = f32[128,4,128]{2,0,1:T(8,128)} async-done(((f32[128,4,128]{2,0,1:T(8,128)}), f32[128,4,128]{2,0,1:T(8,128)}) %all-reduce.4.cloned.1.call-update) | async-done | bytes 262160 | tf_op jit(solution)/shard_map/psum | solution.py:57
  1544.3 129.5 %reduce-scatter.2.cloned.1.call-done = f32[8,4,128]{2,0,1:T(8,128)} async-done(((f32[256,4,128]{2,0,1:T(8,128)}), f32[8,4,128]{2,0,1:T(8,128)}) %reduce-scatter.2.cloned.1.call-update) | async-done | bytes 16400 | tf_op jit(solution)/shard_map/reduce_scatter | solution.py:56
  1673.8 0.7 add_bitcast_fusion
  1674.5 0.0 copy-done.3
  1674.6 0.3 fusion.1
  1674.9 49.9 %all-reduce.1 = (f32[48,48]{0,1:T(8,128)S(1)}, f32[48,48]{0,1:T(8,128)S(1)}) all-reduce(f32[48,48]{0,1:T(8,128)S(1)} %fusion.3, f32[48,48]{0,1:T(8,128)S(1)} %fusion.1), channel_id=1, replica_groups=mesh['row'=32,'col'=16] {'col'}, use_global_device_ids=true, to_apply=%region_0.1 | all-reduce | flops 4608 | bytes 36864 | tf_op jit(solution)/shard_map/psum | solution.py:64
  1724.8 142.5 %all-reduce = (f32[48,48]{0,1:T(8,128)S(1)}, f32[48,48]{0,1:T(8,128)S(1)}) all-reduce(f32[48,48]{0,1:T(8,128)S(1)} %get-tuple-element.16, f32[48,48]{0,1:T(8,128)S(1)} %get-tuple-element.17), channel_id=1, replica_groups=mesh['row'=32,'col'=16] {'row'}, use_global_device_ids=true, to_apply=%region_1.2 | all-reduce | flops 4608 | bytes 36864 | tf_op jit(solution)/shard_map/psum | solution.py:63
  1867.3 0.1 copy.20
  1867.4 4.4 cholesky.18
  1871.8 0.6 compare_reduce_fusion
  1872.5 0.7 fusion.10
  1873.1 3.7 custom-call.12
  1876.8 1.1 fusion
  1877.8 1.0 fusion.2
  1878.9 0.2 convolution_bitcast_fusion.1
  1879.1 0.2 convolution_bitcast_fusion
  1879.3 0.7 copy.28
  (9 shorter events, 0.1 us)
Async XLA Ops:
  7.2 1402.9 %copy-start = (bf16[24,128,128]{2,1,0:T(8,128)(2,1)S(1)}, bf16[24,128,128]{2,1,0:T(8,128)(2,1)}, u32[]{:S(2)}) copy-start(bf16[24,128,128]{2,1,0:T(8,128)(2,1)} %param.10) | copy-start | bytes 2359300
  7.2 1394.9 %all-gather.2.cloned.1.call-start = ((), (), s32[]{:S(2)}) async-start(), calls=%async_computation.1 | async-start | bytes 4202496 | tf_op jit(solution)/shard_map/all_gather | solution.py:32
  7.9 1536.4 %all-reduce.4.cloned.1.call-start = ((), (), s32[]{:S(2)}) async-start(), calls=%async_computation.2 | async-start | bytes 524288 | tf_op jit(solution)/shard_map/psum | solution.py:57
  1405.7 1.9 copy-start.1
  1405.7 9.5 copy-start.4
  1405.7 9.5 copy-start.2
  1405.7 268.8 %copy-start.3 = (f32[44,1024]{1,0:T(8,128)S(1)}, f32[44,1024]{1,0:T(8,128)}, u32[]{:S(2)}) copy-start(f32[44,1024]{1,0:T(8,128)} %param.15) | copy-start | bytes 540676
  1411.8 262.0 %reduce-scatter.2.cloned.1.call-start = ((), (), s32[]{:S(2)}) async-start(), calls=%async_computation.3 | async-start | bytes 540672 | tf_op jit(solution)/shard_map/reduce_scatter | solution.py:56
Sparse Core Ops, SparseCore 0:
  10.2 1391.8 all-gather.1
  1411.9 132.4 all-reduce.3
  1549.6 124.1 reduce-scatter.1

commit v2 on v0

--- a/solution.py
+++ b/solution.py
@@ -54,7 +54,8 @@
     row_partial = place_blocks(local_rows, row_blocks, forward)
     col_partial = place_blocks(local_cols, col_blocks, backward)
     col_share = lax.psum_scatter(col_partial, "row", scatter_dimension=0, tiled=True)
-    row_total = lax.psum(row_partial, "col")
+    pieces = lax.all_gather(row_partial, "col")
+    row_total = jnp.sum(pieces, axis=0)
     own_rows = lax.dynamic_slice_in_dim(row_total, col_index * blocks_dev, blocks_dev, 0)
     new_image = (own_rows + col_share).transpose(1, 0, 2).reshape(vec_count, piece_width)
     trial_wide = trial_vectors.astype(jnp.float32)

time: 1800 us -> 1740 us (0.967)
  waiting for transfers between devices: 1650 us -> 1590 us
    psum x1 -> x0, waiting for transfers between devices: 129 us -> none  [local(): row_total = lax.psum(row_partial, 'col')]
    all_gather x0 -> x1, waiting for transfers between devices: none -> 69.2 us  [local(): pieces = lax.all_gather(row_partial, 'col')]
where the time goes in v2:
time: 1740 us
  waiting for transfers between devices  1590 us (91%)
  blocking collectives  102 us (6%)
    all_gather x1, waiting for transfers between devices, local(): gathered = lax.all_gather(trial_vectors, ('row', 'col'), axis=1, tiled=True)  1390 us
    reduce_scatter x1, waiting for transfers between devices, local(): lax.psum_scatter(col_partial, 'row', scatter_dimension=0, tiled=True)  126 us
    psum x1, blocking collectives, local(): lax.psum((rows_product(basis_all, basis_all), rows_product(basis_all, ima...  102 us
    all_gather x1, waiting for transfers between devices, local(): pieces = lax.all_gather(row_partial, 'col')  69.2 us
  transfers between devices with their start and end apart: 3, of which 3 were waited for; matrix products, arithmetic and copies ran while one was open for 0% of the time, Pallas kernels for 0%

profile of v2, /device:TPU:1, one launch (start us, length us, event | category | flops | bytes accessed | tf_op | source)
XLA Modules:
  0.0 1735.1 jit_solution(8665098735271536829)
XLA Ops:
  7.2 0.0 copy-start
  7.2 0.0 all-gather.4.cloned.1.call-start
  7.2 0.7 all-gather.4.cloned.1.call-update
  7.9 0.0 all-gather.6.cloned.1.call-start
  8.0 0.7 compare_and_fusion
  8.7 1393.4 %all-gather.4.cloned.1.call-done = bf16[4,524288]{1,0:T(4,128)(2,1)} async-done(((bf16[4,1024]{1,0:T(4,128)(2,1)}), bf16[4,524288]{1,0:T(4,128)(2,1)}) %all-gather.4.cloned.1.call-update) | async-done | bytes 4194320 | tf_op jit(solution)/shard_map/all_gather | solution.py:32
  1402.1 3.6 copy.35
  1405.7 0.0 copy-start.1
  1405.7 0.0 copy-start.4
  1405.7 0.0 copy-start.2
  1405.7 1.9 copy-done.1
  1407.7 1.5 dynamic-slice_reduce_fusion
  1409.2 0.1 reshape_reshape.6
  1409.3 0.2 copy.22
  1409.5 0.6 gather_fusion
  1410.1 0.0 copy-done
  1410.2 0.5 fusion.13
  1410.7 0.0 copy-start.3
  1410.7 1.1 fusion.7
  1411.8 0.0 all-gather.6.cloned.1.call-update
  1411.8 0.0 reduce-scatter.2.cloned.1.call-start
  1411.9 0.9 dynamic-slice_bitcast_fusion
  1412.8 0.1 reshape_reshape.7
  1412.9 0.1 copy.25
  1413.0 0.6 gather_fusion.1
  1413.6 0.4 fusion.11
  1414.0 1.3 fusion.4
  1415.3 0.0 reduce-scatter.2.cloned.1.call-update
  1415.3 0.0 copy-done.4
  1415.3 0.0 copy-done.2
  1415.3 0.3 fusion.3
  1415.6 69.2 %all-gather.6.cloned.1.call-done = f32[2048,4,128]{2,0,1:T(8,128)} async-done(((f32[128,4,128]{2,0,1:T(8,128)}), f32[2048,4,128]{2,0,1:T(8,128)}) %all-gather.6.cloned.1.call-update) | async-done | bytes 4194320 | tf_op jit(solution)/shard_map/all_gather | solution.py:57
  1484.8 2.4 reduce_sum.9
  1487.2 125.6 %reduce-scatter.2.cloned.1.call-done = f32[8,4,128]{2,0,1:T(8,128)} async-done(((f32[256,4,128]{2,0,1:T(8,128)}), f32[8,4,128]{2,0,1:T(8,128)}) %reduce-scatter.2.cloned.1.call-update) | async-done | bytes 16400 | tf_op jit(solution)/shard_map/reduce_scatter | solution.py:56
  1612.8 0.7 add_bitcast_fusion
  1613.6 0.0 copy-done.3
  1613.6 0.3 fusion.1
  1613.9 102.0 %all-reduce = (f32[48,48]{0,1:T(8,128)S(1)}, f32[48,48]{0,1:T(8,128)S(1)}) all-reduce(f32[48,48]{0,1:T(8,128)S(1)} %fusion.3, f32[48,48]{0,1:T(8,128)S(1)} %fusion.1), channel_id=1, replica_groups=mesh['row'=32,'col'=16] {'row','col'}, use_global_device_ids=true, to_apply=%region_0.1 | all-reduce | flops 4608 | bytes 36864 | tf_op jit(solution)/shard_map/psum | solution.py:64
  1715.9 0.1 copy.20
  1716.0 4.4 cholesky.18
  1720.4 0.6 compare_reduce_fusion
  1721.0 0.7 fusion.10
  1721.7 3.7 custom-call.12
  1725.4 1.1 fusion.2
  1726.4 1.0 fusion
  1727.5 0.2 convolution_bitcast_fusion.1
  1727.7 0.2 convolution_bitcast_fusion
  1727.9 0.7 copy.28
  (9 shorter events, 0.1 us)
Async XLA Ops:
  7.2 1403.0 %copy-start = (bf16[24,128,128]{2,1,0:T(8,128)(2,1)S(1)}, bf16[24,128,128]{2,1,0:T(8,128)(2,1)}, u32[]{:S(2)}) copy-start(bf16[24,128,128]{2,1,0:T(8,128)(2,1)} %param.10) | copy-start | bytes 2359300
  7.2 1394.9 %all-gather.4.cloned.1.call-start = ((), (), s32[]{:S(2)}) async-start(), calls=%async_computation.1 | async-start | bytes 4202496 | tf_op jit(solution)/shard_map/all_gather | solution.py:32
  7.9 1476.9 %all-gather.6.cloned.1.call-start = ((), (), s32[]{:S(2)}) async-start(), calls=%async_computation.3 | async-start | bytes 4456448 | tf_op jit(solution)/shard_map/all_gather | solution.py:57
  1405.7 2.0 copy-start.1
  1405.7 9.6 copy-start.4
  1405.7 9.6 copy-start.2
  1410.7 202.9 %copy-start.3 = (f32[44,1024]{1,0:T(8,128)S(1)}, f32[44,1024]{1,0:T(8,128)}, u32[]{:S(2)}) copy-start(f32[44,1024]{1,0:T(8,128)} %param.15) | copy-start | bytes 540676
  1411.8 201.0 %reduce-scatter.2.cloned.1.call-start = ((), (), s32[]{:S(2)}) async-start(), calls=%async_computation.2 | async-start | bytes 540672 | tf_op jit(solution)/shard_map/reduce_scatter | solution.py:56
Sparse Core Ops, SparseCore 0:
  10.2 1391.8 all-gather.3
  1411.9 72.8 all-gather.5
  1489.4 123.3 reduce-scatter.1
